TPU v7x, 32 devices: a whole 2x2x4 slice. The times are simulated.
32 devices in a mesh: groups: 2 (over y), expert: 8 (over z, x), section: 2 (over core).
Axes of the slice: x: 2, y: 2, z: 4, core: 2. Of those that a mesh axis runs over, the one named last changes fastest.
Arguments:
- tokens: bfloat16 [2, 128, 7168], P(None, ('groups', 'expert')), parts along dimension 1, may hold values from -6 to 6
- routes: int32 [2, 2, 128, 4], P('section', None, ('groups', 'expert')), parts along dimension 2, may hold values from 0 to 15, all different within a row; in each aligned block of 8 rows (0 to 7, 8 to 15, ..., all dimensions but the last counted through in order) at most 3 rows name the same one
- norm_gain: float32 [2, 7168], P('section'), may hold values from 0.5 to 1.5
- router_weight: bfloat16 [2, 7168, 16], P('section'), may hold values from -0.125 to 0.125
- gate_weight: bfloat16 [2, 7168, 16384], P('section', None, 'expert'), may hold values from -0.0625 to 0.0625
- up_weight: bfloat16 [2, 7168, 16384], P('section', None, 'expert'), may hold values from -0.0625 to 0.0625
- down_weight: bfloat16 [2, 16384, 7168], P('section', 'expert'), may hold values from -0.375 to 0.375
Outputs:
- encoded: bfloat16 [2, 128, 7168], P('section', ('groups', 'expert')), parts along dimension 1
There are 2 independent parts, one for each index of `groups`. A program takes and returns all parts, laid end to end along the dimension named above; an argument that names none is the same for every part. Nothing has to cross between parts.
Inputs may be any that keep to these rules, and one draw needn't show every extreme that they name: `routes`: each token names 4 different experts. For every layer, micro-batch and aligned block of 8 tokens, no expert is named by more than 3 of the block's tokens.
All inputs are finite; a program needn't handle non-finite values.
Results may differ from a plain program's by a relative error of at most 0.0074.
Values may be sent and summed in bfloat16 or wider, within the bound.
A program may use at most 256 MiB of HBM per device.

v0:
```python
import functools

import jax
import jax.numpy as jnp
from jax import lax
from jax.experimental import pallas as pl
from jax.experimental.pallas import tpu as pltpu
from jax.sharding import PartitionSpec as P

EPSILON = 1e-06
MESH = pl.DeviceIdType.MESH
LANES = 128


def largest_divisor(value, most):
    return next(d for d in range(min(value, most), 0, -1) if value % d == 0)


def kernel(
    count, unit_width, slots_gu, slots_d,
    tokens, hit, gain, router, gate_hbm, up_hbm, down_hbm, out,
    x, g, gates, hidden, wgu, wd, y, rx, rz, res, fin,
    sem_gu, sem_d, gather_send, gather_recv, fwd_send, fwd_recv,
    pair_send, pair_recv, line_send, line_recv, pass_send, pass_recv,
):
    me = lax.axis_index("expert")
    sec = lax.axis_index("section")
    line = count // 2
    col, pos = lax.rem(me, 2), lax.div(me, 2)
    other = 1 - col
    width = x.shape[-1]
    tile_f = wgu.shape[-1]
    tile_d = wd.shape[-1]
    ff_local = hidden.shape[-1]
    steps_f = ff_local // tile_f
    steps_d = width // tile_d
    rows = g.shape[2]
    total = count * rows
    half = rows // 2
    partner = {"expert": pos * 2 + other}
    across = {"section": 1 - sec}

    def member(p):
        return {"expert": p * 2 + col}

    def load_gu(f, which, start):
        slot = lax.rem(f, slots_gu)
        source = (gate_hbm, up_hbm)[which]
        copy = pltpu.make_async_copy(
            source.at[0, :, pl.ds(pl.multiple_of(f * tile_f, tile_f), tile_f)],
            wgu.at[slot, which],
            sem_gu.at[slot, which],
        )
        copy.start() if start else copy.wait()

    def load_d(c, start):
        slot = lax.rem(c, slots_d)
        copy = pltpu.make_async_copy(
            down_hbm.at[0, :, pl.ds(pl.multiple_of(c * tile_d, tile_d), tile_d)],
            wd.at[slot],
            sem_d.at[slot],
        )
        copy.start() if start else copy.wait()

    for f in range(slots_gu):
        load_gu(f, 0, True)
        load_gu(f, 1, True)
    for c in range(slots_d):
        load_d(c, True)

    barrier = pltpu.get_barrier_semaphore()
    for k in range(1, line):
        pl.semaphore_signal(barrier, inc=1, device_id=member(lax.rem(pos + k, line)), device_id_type=MESH)
    pl.semaphore_signal(barrier, inc=1, device_id=partner, device_id_type=MESH)
    pl.semaphore_signal(barrier, inc=1, device_id=across, device_id_type=MESH)
    pl.semaphore_wait(barrier, line + 1)

    def remote(src, dst, send, recv, device):
        return pltpu.make_async_remote_copy(
            src_ref=src, dst_ref=dst, send_sem=send, recv_sem=recv,
            device_id=device, device_id_type=MESH,
        )

    def pass_on():
        return remote(res, x, pass_send.at[0], pass_recv.at[0], across)

    def give_back():
        return remote(res.at[0], fin, pass_send.at[1], pass_recv.at[1], across)

    @pl.when(sec == 0)
    def _():
        x[...] = tokens[...]

    @pl.when(sec == 1)
    def _():
        pass_on().wait_recv()

    for m in range(2):
        values = x[m].astype(jnp.float32)
        factor = lax.rsqrt(jnp.mean(values * values, axis=-1, keepdims=True) + EPSILON)
        g[col, pos, m * half:(m + 1) * half, 0:width] = (values * factor * gain[...]).astype(jnp.bfloat16)
    g[col, pos, :, width:width + LANES] = hit[...]

    def to_member(k):
        block = g.at[col, pos]
        return remote(block, block, gather_send.at[k], gather_recv.at[k], member(lax.rem(pos + k, line)))

    def from_member(k):
        block = g.at[col, lax.rem(pos + line - k, line)]
        return remote(block, block, gather_send.at[k], gather_recv.at[k], partner)

    def to_partner(k):
        block = g.at[col, lax.rem(pos + line - k, line)]
        return remote(block, block, fwd_send.at[k], fwd_recv.at[k], partner)

    def from_partner(k):
        block = g.at[other, lax.rem(pos + line - k, line)]
        return remote(block, block, fwd_send.at[k], fwd_recv.at[k], partner)

    to_partner(0).start()
    for k in range(1, line):
        to_member(k).start()
    for k in range(1, line):
        from_member(k).wait_recv()
        to_partner(k).start()
    for k in range(line):
        from_partner(k).wait_recv()

    def all_rows():
        return g[:, :, :, 0:width].reshape(total, width)

    experts = router.shape[-1]
    logits = jnp.dot(all_rows(), router[0], preferred_element_type=jnp.float32)
    routed = g[:, :, :, width:width + LANES].reshape(total, LANES)[:, 0:experts].astype(jnp.float32)
    picked = jax.nn.sigmoid(logits) * routed
    gates[...] = picked / jnp.sum(picked, axis=-1, keepdims=True)

    def up_step(f, carry):
        slot = lax.rem(f, slots_gu)
        load_gu(f, 0, False)
        load_gu(f, 1, False)
        lhs = all_rows()
        gate_part = jnp.dot(lhs, wgu[slot, 0], preferred_element_type=jnp.float32)
        up_part = jnp.dot(lhs, wgu[slot, 1], preferred_element_type=jnp.float32)
        expert = lax.div(me * ff_local + f * tile_f, unit_width)
        lane = lax.broadcasted_iota(jnp.int32, (total, experts), 1)
        scale = jnp.sum(jnp.where(lane == expert, gates[...], 0.0), axis=-1, keepdims=True)
        value = gate_part / (1.0 + jnp.exp(-gate_part)) * up_part * scale
        hidden[:, pl.ds(pl.multiple_of(f * tile_f, tile_f), tile_f)] = value.astype(jnp.bfloat16)

        @pl.when(f + slots_gu < steps_f)
        def _():
            load_gu(f + slots_gu, 0, True)
            load_gu(f + slots_gu, 1, True)

        return carry

    lax.fori_loop(0, steps_f, up_step, 0)

    def pair_copy(c):
        return remote(y.at[c, other], rx.at[c], pair_send.at[c], pair_recv.at[c], partner)

    def line_copy(c, k):
        p = lax.rem(pos + k, line)
        return remote(y.at[c, col, p], rz.at[c, k - 1], line_send.at[c, k - 1], line_recv.at[c, k - 1], member(p))

    def line_step(c):
        pair_copy(c).wait_recv()
        y[c, col] = (y[c, col].astype(jnp.float32) + rx[c].astype(jnp.float32)).astype(jnp.bfloat16)
        for k in range(1, line):
            line_copy(c, k).start()

    def down_step(c, carry):
        load_d(c, False)
        part = jnp.dot(hidden[...], wd[lax.rem(c, slots_d)], preferred_element_type=jnp.float32)
        y[c] = part.astype(jnp.bfloat16).reshape(2, line, rows, tile_d)
        pair_copy(c).start()

        @pl.when(c + slots_d < steps_d)
        def _():
            load_d(c + slots_d, True)

        @pl.when(c >= 1)
        def _():
            line_step(c - 1)

        return carry

    lax.fori_loop(0, steps_d, down_step, 0)
    line_step(steps_d - 1)

    def finish_step(c, carry):
        at = pl.ds(pl.multiple_of(c * tile_d, tile_d), tile_d)
        branch = y[c, col, pos].astype(jnp.float32)
        for k in range(1, line):
            line_copy(c, k).wait_recv()
            branch = branch + rz[c, k - 1].astype(jnp.float32)
        for m in range(2):
            res[m, :, at] = (x[m, :, at].astype(jnp.float32) + branch[m * half:(m + 1) * half]).astype(jnp.bfloat16)
        return carry

    lax.fori_loop(0, steps_d, finish_step, 0)

    @pl.when(sec == 0)
    def _():
        pass_on().start()

    @pl.when(sec == 1)
    def _():
        give_back().start()

    for k in range(1, line):
        to_member(k).wait_send()
    for k in range(line):
        to_partner(k).wait_send()

    def drain_step(c, carry):
        pair_copy(c).wait_send()
        for k in range(1, line):
            line_copy(c, k).wait_send()
        return carry

    lax.fori_loop(0, steps_d, drain_step, 0)

    @pl.when(sec == 0)
    def _():
        pass_on().wait_send()
        give_back().wait_recv()
        out[0] = fin[...]

    @pl.when(sec == 1)
    def _():
        out[0] = res[1]
        give_back().wait_send()


def local(count, tokens, routes, norm_gain, router_weight, gate_weight, up_weight, down_weight):
    micro, per_block, width = tokens.shape
    rows = micro * per_block
    experts = router_weight.shape[-1]
    ff_local = gate_weight.shape[-1]
    unit_width = ff_local * count // experts
    line = count // 2
    tile_f = largest_divisor(min(unit_width, ff_local), 256)
    tile_d = largest_divisor(width, 512)
    steps_f, steps_d = ff_local // tile_f, width // tile_d
    slots_gu, slots_d = min(steps_f, 5), min(steps_d, 6)
    picks = routes[0].reshape(rows, routes.shape[-1])
    hit = jnp.sum(
        (picks[:, :, None] == jnp.arange(LANES, dtype=jnp.int32)).astype(jnp.float32), axis=1
    ).astype(jnp.bfloat16)
    dma = pltpu.SemaphoreType.DMA
    vmem = pl.BlockSpec(memory_space=pltpu.VMEM)
    anyspace = pl.BlockSpec(memory_space=pl.ANY)
    bf16 = jnp.bfloat16
    return pl.pallas_call(
        functools.partial(kernel, count, unit_width, slots_gu, slots_d),
        out_shape=jax.ShapeDtypeStruct((1, per_block, width), bf16),
        in_specs=[vmem, vmem, vmem, vmem, anyspace, anyspace, anyspace],
        out_specs=vmem,
        scratch_shapes=[
            pltpu.VMEM((micro, per_block, width), bf16),
            pltpu.VMEM((2, line, rows, width + LANES), bf16),
            pltpu.VMEM((count * rows, experts), jnp.float32),
            pltpu.VMEM((count * rows, ff_local), bf16),
            pltpu.VMEM((slots_gu, 2, width, tile_f), bf16),
            pltpu.VMEM((slots_d, ff_local, tile_d), bf16),
            pltpu.VMEM((steps_d, 2, line, rows, tile_d), bf16),
            pltpu.VMEM((steps_d, line, rows, tile_d), bf16),
            pltpu.VMEM((steps_d, line - 1, rows, tile_d), bf16),
            pltpu.VMEM((micro, per_block, width), bf16),
            pltpu.VMEM((per_block, width), bf16),
            dma((slots_gu, 2)),
            dma((slots_d,)),
            dma((line,)),
            dma((line,)),
            dma((line,)),
            dma((line,)),
            dma((steps_d,)),
            dma((steps_d,)),
            dma((steps_d, line - 1)),
            dma((steps_d, line - 1)),
            dma((2,)),
            dma((2,)),
        ],
        compiler_params=pltpu.CompilerParams(
            collective_id=0, has_side_effects=True, vmem_limit_bytes=67043328
        ),
    )(tokens, hit, norm_gain, router_weight, gate_weight, up_weight, down_weight)


def solution(mesh):
    placed = (
        P(None, ("groups", "expert"), None),
        P("section", None, ("groups", "expert"), None),
        P("section", None),
        P("section", None, None),
        P("section", None, "expert"),
        P("section", None, "expert"),
        P("section", "expert", None),
    )
    return jax.shard_map(
        functools.partial(local, mesh.shape["expert"]),
        mesh=mesh,
        in_specs=placed,
        out_specs=P("section", ("groups", "expert"), None),
        check_vma=False,
    )
```

profile of v0, /device:TPU:0, one launch (start us, length us, event | category | flops | bytes accessed | tf_op | source)
XLA Modules:
  0.0 130.6 jit_solution(17766222789869445731)
XLA Ops:
  0.0 0.7 copy.11
  0.7 0.1 eq.15
  0.8 0.7 convert_reduce_fusion.hit
  1.4 2.5 %copy.12.router = bf16[1,7168,16]{2,1,0:T(8,128)(2,1)} copy(bf16[1,7168,16]{1,2,0:T(8,128)(2,1)} %param.10) | data formatting | bytes 458752 | tf_op args[3]
  4.0 125.1 %shard_map.73 = bf16[1,8,7168]{2,1,0:T(8,128)(2,1)} custom-call(bf16[2,8,7168]{2,1,0:T(8,128)(2,1)} %tokens.1, bf16[16,128]{1,0:T(8,128)(2,1)} %convert_reduce_fusion.hit, f32[1,7168]{1,0:T(1,128)} %gain.1, bf16[1,7168,16]{2,1,0:T(8,128)(2,1)} %copy.12.router, bf16[1,7168,2048]{2,1,0:T(8,128)(2,1)} %gate_hbm.1, bf16[1,7168,2048]{2,1,0:T(8,128)(2,1)} %up_hbm.1, ...), custom_call_target="tpu_custom_call" | custom-call | tf_op jit(solution)/shard_map/pallas_call | solution.py:256
  129.1 1.6 %copy.14 = bf16[1,8,7168]{2,1,0:T(8,128)(2,1)} copy(bf16[1,8,7168]{2,1,0:T(8,128)(2,1)} %shard_map.73) | data formatting | bytes 229376
where the time goes:
time: 131 us
  Pallas kernels  125 us (95%)
  local copies, waits for them, and re-layouts  4.83 us (4%)
    pallas_call x1, Pallas kernels, local(): pl.pallas_call(functools.partial(kernel, count, unit_width, slots_gu, slo...  125 us
    unnamed x3, local copies, waits for them, and re-layouts  4.74 us

commit v1 on v0

v1 whole, which is shorter than its diff:
```python
import functools

import jax
import jax.numpy as jnp
from jax import lax
from jax.experimental import pallas as pl
from jax.experimental.pallas import tpu as pltpu
from jax.sharding import PartitionSpec as P

EPSILON = 1e-06
MESH = pl.DeviceIdType.MESH
LANES = 128
LAG = 5
AHEAD = 2


def largest_divisor(value, most):
    return next(d for d in range(min(value, most), 0, -1) if value % d == 0)


def kernel(
    count, unit_width, slots_gu, slots_d,
    tokens, hit, gain, router, gate_hbm, up_hbm, down_hbm, out,
    x, g, marks, logits, acc, hidden, wgu, wd, y, rx, rz, res, fin,
    sem_gu, sem_d, gather_send, gather_recv, fwd_send, fwd_recv,
    pair_send, pair_recv, line_send, line_recv, pass_send, pass_recv,
):
    me = lax.axis_index("expert")
    sec = lax.axis_index("section")
    line = count // 2
    col, pos = lax.rem(me, 2), lax.div(me, 2)
    other = 1 - col
    width = x.shape[-1]
    tile_k = wgu.shape[1]
    tile_f = largest_divisor(min(unit_width, wgu.shape[-1]), 512)
    steps_k = width // tile_k
    tile_d = wd.shape[-1]
    ff_local = hidden.shape[-1]
    steps_f = ff_local // tile_f
    loads = 2 * steps_k
    steps_d = width // tile_d
    rows = g.shape[3]
    total = count * rows
    half = rows // 2
    partner = {"expert": pos * 2 + other}
    across = {"section": 1 - sec}

    def member(p):
        return {"expert": p * 2 + col}

    def load_gu(k, which, start):
        slot = lax.rem(2 * k + which, slots_gu)
        source = (gate_hbm, up_hbm)[which]
        copy = pltpu.make_async_copy(
            source.at[0, pl.ds(pl.multiple_of(k * tile_k, tile_k), tile_k), :],
            wgu.at[slot],
            sem_gu.at[slot],
        )
        copy.start() if start else copy.wait()

    def load_d(c, start):
        slot = lax.rem(c, slots_d)
        copy = pltpu.make_async_copy(
            down_hbm.at[0, :, pl.ds(pl.multiple_of(c * tile_d, tile_d), tile_d)],
            wd.at[slot],
            sem_d.at[slot],
        )
        copy.start() if start else copy.wait()

    for number in range(slots_gu):
        load_gu(number // 2, number % 2, True)

    def first_down():
        for c in range(slots_d):
            load_d(c, True)

    @pl.when(sec == 1)
    def _():
        first_down()

    barrier = pltpu.get_barrier_semaphore()
    for k in range(1, line):
        pl.semaphore_signal(barrier, inc=1, device_id=member(lax.rem(pos + k, line)), device_id_type=MESH)
    pl.semaphore_signal(barrier, inc=1, device_id=partner, device_id_type=MESH)
    pl.semaphore_signal(barrier, inc=1, device_id=across, device_id_type=MESH)
    pl.semaphore_wait(barrier, line + 1)

    def remote(src, dst, send, recv, device):
        return pltpu.make_async_remote_copy(
            src_ref=src, dst_ref=dst, send_sem=send, recv_sem=recv,
            device_id=device, device_id_type=MESH,
        )

    def pass_on():
        return remote(res, x, pass_send.at[0], pass_recv.at[0], across)

    def give_back():
        return remote(res.at[0], fin, pass_send.at[1], pass_recv.at[1], across)

    def block_of(k, c, p):
        return g.at[k, c, p] if k is not None else marks.at[c, p]

    def sem_of(k):
        return k if k is not None else steps_k

    def to_member(k, j):
        block = block_of(k, col, pos)
        return remote(block, block, gather_send.at[sem_of(k), j], gather_recv.at[sem_of(k), j], member(lax.rem(pos + j, line)))

    def from_member(k, j):
        block = block_of(k, col, lax.rem(pos + line - j, line))
        return remote(block, block, gather_send.at[sem_of(k), j], gather_recv.at[sem_of(k), j], partner)

    def to_partner(k, j):
        block = block_of(k, col, lax.rem(pos + line - j, line))
        return remote(block, block, fwd_send.at[sem_of(k), j], fwd_recv.at[sem_of(k), j], partner)

    def from_partner(k, j):
        block = block_of(k, other, lax.rem(pos + line - j, line))
        return remote(block, block, fwd_send.at[sem_of(k), j], fwd_recv.at[sem_of(k), j], partner)

    def send_own(k):
        for j in range(1, line):
            to_member(k, j).start()
        to_partner(k, 0).start()

    def forward(k):
        for j in range(1, line):
            from_member(k, j).wait_recv()
            to_partner(k, j).start()

    def receive(k):
        for j in range(line):
            from_partner(k, j).wait_recv()

    marks[col, pos] = hit[...]
    send_own(None)

    @pl.when(sec == 0)
    def _():
        x[...] = tokens[...]

    @pl.when(sec == 1)
    def _():
        pass_on().wait_recv()

    factors = []
    for m in range(2):
        values = x[m].astype(jnp.float32)
        factors.append(lax.rsqrt(jnp.mean(values * values, axis=-1, keepdims=True) + EPSILON))
    for k in range(steps_k):
        for m in range(2):
            values = x[m, :, k * tile_k:(k + 1) * tile_k].astype(jnp.float32)
            normed = values * factors[m] * gain[:, k * tile_k:(k + 1) * tile_k]
            g[k, col, pos, m * half:(m + 1) * half, :] = normed.astype(jnp.bfloat16)
        send_own(k)

    experts = router.shape[1]
    acc[...] = jnp.zeros_like(acc)
    logits[...] = jnp.zeros_like(logits)
    forward(None)
    ahead = min(steps_k, AHEAD)
    for k in range(ahead):
        forward(k)

    def up_step(k, carry):
        @pl.when(k + ahead < steps_k)
        def _():
            forward(k + ahead)

        receive(k)
        lhs = g[k].reshape(total, tile_k)
        at = pl.ds(pl.multiple_of(k * tile_k, tile_k), tile_k)
        logits[...] += lax.dot_general(
            lhs, router[0, :, at], (((1,), (1,)), ((), ())), preferred_element_type=jnp.float32
        )
        for which in range(2):
            load_gu(k, which, False)
            slot = lax.rem(2 * k + which, slots_gu)
            for f in range(steps_f):
                cut = slice(f * tile_f, (f + 1) * tile_f)
                acc[which, :, cut] += jnp.dot(lhs, wgu[slot, :, cut], preferred_element_type=jnp.float32)
            later = 2 * k + which + slots_gu

            @pl.when(later < loads)
            def _():
                if slots_gu % 2 == 0:
                    load_gu(k + slots_gu // 2, which, True)
                elif which == 0:
                    load_gu(k + slots_gu // 2, 1, True)
                else:
                    load_gu(k + slots_gu // 2 + 1, 0, True)

        @pl.when((sec == 0) & (k == start_down))
        def _():
            first_down()

        return carry

    start_down = max(0, (loads - slots_gu - 1) // 2)
    lax.fori_loop(0, steps_k, up_step, 0)

    receive(None)
    routed = marks[...].reshape(total, LANES)[:, 0:experts].astype(jnp.float32)
    picked = jax.nn.sigmoid(logits[...]) * routed
    gates = picked / jnp.sum(picked, axis=-1, keepdims=True)
    lane = lax.broadcasted_iota(jnp.int32, (total, experts), 1)
    for f in range(steps_f):
        cut = slice(f * tile_f, (f + 1) * tile_f)
        expert = lax.div(me * ff_local + f * tile_f, unit_width)
        scale = jnp.sum(jnp.where(lane == expert, gates, 0.0), axis=-1, keepdims=True)
        gate_part = acc[0, :, cut]
        value = gate_part / (1.0 + jnp.exp(-gate_part)) * acc[1, :, cut] * scale
        hidden[:, cut] = value.astype(jnp.bfloat16)

    def pair_copy(c):
        return remote(y.at[c, other], rx.at[c], pair_send.at[c], pair_recv.at[c], partner)

    def line_copy(c, k):
        p = lax.rem(pos + k, line)
        return remote(y.at[c, col, p], rz.at[c, k - 1], line_send.at[c, k - 1], line_recv.at[c, k - 1], member(p))

    def line_step(c):
        pair_copy(c).wait_recv()
        y[c, col] = (y[c, col].astype(jnp.float32) + rx[c].astype(jnp.float32)).astype(jnp.bfloat16)
        for k in range(1, line):
            line_copy(c, k).start()

    def down_step(c, carry):
        load_d(c, False)
        part = jnp.dot(hidden[...], wd[lax.rem(c, slots_d)], preferred_element_type=jnp.float32)
        y[c] = part.astype(jnp.bfloat16).reshape(2, line, rows, tile_d)
        pair_copy(c).start()

        @pl.when(c + slots_d < steps_d)
        def _():
            load_d(c + slots_d, True)

        @pl.when(c >= lag_d)
        def _():
            line_step(c - lag_d)

        return carry

    def late_step(c, carry):
        line_step(c)
        return carry

    lag_d = min(steps_d, LAG)
    lax.fori_loop(0, steps_d, down_step, 0)
    lax.fori_loop(steps_d - lag_d, steps_d, late_step, 0)

    def finish_step(c, carry):
        at = pl.ds(pl.multiple_of(c * tile_d, tile_d), tile_d)
        branch = y[c, col, pos].astype(jnp.float32)
        for k in range(1, line):
            line_copy(c, k).wait_recv()
            branch = branch + rz[c, k - 1].astype(jnp.float32)
        for m in range(2):
            res[m, :, at] = (x[m, :, at].astype(jnp.float32) + branch[m * half:(m + 1) * half]).astype(jnp.bfloat16)
        return carry

    lax.fori_loop(0, steps_d, finish_step, 0)

    @pl.when(sec == 0)
    def _():
        pass_on().start()

    @pl.when(sec == 1)
    def _():
        give_back().start()

    def drain_own(k):
        for j in range(1, line):
            to_member(k, j).wait_send()
        for j in range(line):
            to_partner(k, j).wait_send()

    def drain_chunk(k, carry):
        drain_own(k)
        return carry

    drain_own(None)
    lax.fori_loop(0, steps_k, drain_chunk, 0)

    def drain_step(c, carry):
        pair_copy(c).wait_send()
        for k in range(1, line):
            line_copy(c, k).wait_send()
        return carry

    lax.fori_loop(0, steps_d, drain_step, 0)

    @pl.when(sec == 0)
    def _():
        pass_on().wait_send()
        give_back().wait_recv()
        out[0] = fin[...]

    @pl.when(sec == 1)
    def _():
        out[0] = res[1]
        give_back().wait_send()


def local(count, tokens, routes, norm_gain, router_weight, gate_weight, up_weight, down_weight):
    micro, per_block, width = tokens.shape
    rows = micro * per_block
    experts = router_weight.shape[-1]
    ff_local = gate_weight.shape[-1]
    unit_width = ff_local * count // experts
    line = count // 2
    tile_k = largest_divisor(width, 1024)
    tile_d = largest_divisor(width, 512)
    steps_k, steps_d = width // tile_k, width // tile_d
    slots_gu, slots_d = min(2 * steps_k, 9), min(steps_d, 6)
    picks = routes[0].reshape(rows, routes.shape[-1])
    hit = jnp.sum(
        (picks[:, :, None] == jnp.arange(LANES, dtype=jnp.int32)).astype(jnp.float32), axis=1
    ).astype(jnp.bfloat16)
    dma = pltpu.SemaphoreType.DMA
    vmem = pl.BlockSpec(memory_space=pltpu.VMEM)
    anyspace = pl.BlockSpec(memory_space=pl.ANY)
    bf16 = jnp.bfloat16
    return pl.pallas_call(
        functools.partial(kernel, count, unit_width, slots_gu, slots_d),
        out_shape=jax.ShapeDtypeStruct((1, per_block, width), bf16),
        in_specs=[vmem, vmem, vmem, vmem, anyspace, anyspace, anyspace],
        out_specs=vmem,
        scratch_shapes=[
            pltpu.VMEM((micro, per_block, width), bf16),
            pltpu.VMEM((steps_k, 2, line, rows, tile_k), bf16),
            pltpu.VMEM((2, line, rows, LANES), bf16),
            pltpu.VMEM((count * rows, experts), jnp.float32),
            pltpu.VMEM((2, count * rows, ff_local), jnp.float32),
            pltpu.VMEM((count * rows, ff_local), bf16),
            pltpu.VMEM((slots_gu, tile_k, ff_local), bf16),
            pltpu.VMEM((slots_d, ff_local, tile_d), bf16),
            pltpu.VMEM((steps_d, 2, line, rows, tile_d), bf16),
            pltpu.VMEM((steps_d, line, rows, tile_d), bf16),
            pltpu.VMEM((steps_d, line - 1, rows, tile_d), bf16),
            pltpu.VMEM((micro, per_block, width), bf16),
            pltpu.VMEM((per_block, width), bf16),
            dma((slots_gu,)),
            dma((slots_d,)),
            dma((steps_k + 1, line)),
            dma((steps_k + 1, line)),
            dma((steps_k + 1, line)),
            dma((steps_k + 1, line)),
            dma((steps_d,)),
            dma((steps_d,)),
            dma((steps_d, line - 1)),
            dma((steps_d, line - 1)),
            dma((2,)),
            dma((2,)),
        ],
        compiler_params=pltpu.CompilerParams(
            collective_id=0, has_side_effects=True, vmem_limit_bytes=67043328
        ),
    )(tokens, hit, norm_gain, jnp.swapaxes(router_weight, 1, 2), gate_weight, up_weight, down_weight)


def solution(mesh):
    placed = (
        P(None, ("groups", "expert"), None),
        P("section", None, ("groups", "expert"), None),
        P("section", None),
        P("section", None, None),
        P("section", None, "expert"),
        P("section", None, "expert"),
        P("section", "expert", None),
    )
    return jax.shard_map(
        functools.partial(local, mesh.shape["expert"]),
        mesh=mesh,
        in_specs=placed,
        out_specs=P("section", ("groups", "expert"), None),
        check_vma=False,
    )
```

time: 131 us -> 86 us (0.66)
  Pallas kernels: 125 us -> 82.8 us
  local copies, waits for them, and re-layouts: 4.83 us -> 2.33 us
    pallas_call x1, Pallas kernels: 125 us -> 82.8 us  [local(): pl.pallas_call(functools.partial(kernel, count, unit_width, slots_gu, slo...]
    unnamed x3 -> x2, local copies, waits for them, and re-layouts: 4.74 us -> 2.24 us
where the time goes in v1:
time: 86 us; the launch traced here: 85.8 us
  Pallas kernels  82.8 us (96%)
  local copies, waits for them, and re-layouts  2.33 us (3%)
    pallas_call x1, Pallas kernels, local(): pl.pallas_call(functools.partial(kernel, count, unit_width, slots_gu, slo...  82.8 us
    unnamed x2, local copies, waits for them, and re-layouts  2.24 us

profile of v1, /device:TPU:0, one launch (start us, length us, event | category | flops | bytes accessed | tf_op | source)
XLA Modules:
  0.0 85.8 jit_solution(3453395614843869500)
XLA Ops:
  0.0 0.7 copy.10
  0.7 0.1 eq.15
  0.8 0.7 convert_reduce_fusion.hit
  1.4 82.8 %shard_map.73 = bf16[1,8,7168]{2,1,0:T(8,128)(2,1)} custom-call(bf16[2,8,7168]{2,1,0:T(8,128)(2,1)} %tokens.1, bf16[16,128]{1,0:T(8,128)(2,1)} %convert_reduce_fusion.hit, f32[1,7168]{1,0:T(1,128)} %gain.1, bf16[1,16,7168]{2,1,0:T(8,128)(2,1)} %bitcast.3, bf16[1,7168,2048]{2,1,0:T(8,128)(2,1)} %gate_hbm.1, bf16[1,7168,2048]{2,1,0:T(8,128)(2,1)} %up_hbm.1, ...), custom_call_target="tpu_custom_call" | custom-call | tf_op jit(solution)/shard_map/pallas_call | solution.py:325
  84.2 1.6 %copy.12 = bf16[1,8,7168]{2,1,0:T(8,128)(2,1)} copy(bf16[1,8,7168]{2,1,0:T(8,128)(2,1)} %shard_map.73) | data formatting | bytes 229376

commit v2 on v1

--- a/solution.py
+++ b/solution.py
@@ -91,11 +91,23 @@
             device_id=device, device_id_type=MESH,
         )
 
-    def pass_on():
-        return remote(res, x, pass_send.at[0], pass_recv.at[0], across)
-
-    def give_back():
-        return remote(res.at[0], fin, pass_send.at[1], pass_recv.at[1], across)
+    def columns(c):
+        return pl.ds(pl.multiple_of(c * tile_d, tile_d), tile_d)
+
+    def pass_on(c):
+        cut = columns(c)
+        return remote(res.at[:, :, cut], x.at[:, :, cut], pass_send.at[0, c], pass_recv.at[0, c], across)
+
+    def give_back(c):
+        cut = columns(c)
+        return remote(res.at[0, :, cut], fin.at[:, cut], pass_send.at[1, c], pass_recv.at[1, c], across)
+
+    def each_column(act):
+        def step(c, carry):
+            act(c)
+            return carry
+
+        lax.fori_loop(0, steps_d, step, 0)
 
     def block_of(k, c, p):
         return g.at[k, c, p] if k is not None else marks.at[c, p]
@@ -142,7 +154,7 @@
 
     @pl.when(sec == 1)
     def _():
-        pass_on().wait_recv()
+        each_column(lambda c: pass_on(c).wait_recv())
 
     factors = []
     for m in range(2):
@@ -251,24 +263,25 @@
     lax.fori_loop(steps_d - lag_d, steps_d, late_step, 0)
 
     def finish_step(c, carry):
-        at = pl.ds(pl.multiple_of(c * tile_d, tile_d), tile_d)
+        at = columns(c)
         branch = y[c, col, pos].astype(jnp.float32)
         for k in range(1, line):
             line_copy(c, k).wait_recv()
             branch = branch + rz[c, k - 1].astype(jnp.float32)
         for m in range(2):
             res[m, :, at] = (x[m, :, at].astype(jnp.float32) + branch[m * half:(m + 1) * half]).astype(jnp.bfloat16)
+
+        @pl.when(sec == 0)
+        def _():
+            pass_on(c).start()
+
+        @pl.when(sec == 1)
+        def _():
+            give_back(c).start()
+
         return carry
 
     lax.fori_loop(0, steps_d, finish_step, 0)
-
-    @pl.when(sec == 0)
-    def _():
-        pass_on().start()
-
-    @pl.when(sec == 1)
-    def _():
-        give_back().start()
 
     def drain_own(k):
         for j in range(1, line):
@@ -293,14 +306,14 @@
 
     @pl.when(sec == 0)
     def _():
-        pass_on().wait_send()
-        give_back().wait_recv()
+        each_column(lambda c: pass_on(c).wait_send())
+        each_column(lambda c: give_back(c).wait_recv())
         out[0] = fin[...]
 
     @pl.when(sec == 1)
     def _():
         out[0] = res[1]
-        give_back().wait_send()
+        each_column(lambda c: give_back(c).wait_send())
 
 
 def local(count, tokens, routes, norm_gain, router_weight, gate_weight, up_weight, down_weight):
@@ -351,8 +364,8 @@
             dma((steps_d,)),
             dma((steps_d, line - 1)),
             dma((steps_d, line - 1)),
-            dma((2,)),
-            dma((2,)),
+            dma((2, steps_d)),
+            dma((2, steps_d)),
         ],
         compiler_params=pltpu.CompilerParams(
             collective_id=0, has_side_effects=True, vmem_limit_bytes=67043328

time: 86 us -> 86 us (level)
  no operation moved by 1% of the time
where the time goes in v2:
time: 86 us; the launch traced here: 85.8 us
  Pallas kernels  82.8 us (96%)
  local copies, waits for them, and re-layouts  2.33 us (3%)
    pallas_call x1, Pallas kernels, local(): pl.pallas_call(functools.partial(kernel, count, unit_width, slots_gu, slo...  82.8 us
    unnamed x2, local copies, waits for them, and re-layouts  2.24 us

profile of v2, /device:TPU:0, one launch (start us, length us, event | category | flops | bytes accessed | tf_op | source)
XLA Modules:
  0.0 85.8 jit_solution(10009335011557121873)
XLA Ops:
  0.0 0.7 copy.10
  0.7 0.1 eq.15
  0.8 0.7 convert_reduce_fusion.hit
  1.4 82.8 %shard_map.73 = bf16[1,8,7168]{2,1,0:T(8,128)(2,1)} custom-call(bf16[2,8,7168]{2,1,0:T(8,128)(2,1)} %tokens.1, bf16[16,128]{1,0:T(8,128)(2,1)} %convert_reduce_fusion.hit, f32[1,7168]{1,0:T(1,128)} %gain.1, bf16[1,16,7168]{2,1,0:T(8,128)(2,1)} %bitcast.3, bf16[1,7168,2048]{2,1,0:T(8,128)(2,1)} %gate_hbm.1, bf16[1,7168,2048]{2,1,0:T(8,128)(2,1)} %up_hbm.1, ...), custom_call_target="tpu_custom_call" | custom-call | tf_op jit(solution)/shard_map/pallas_call | solution.py:338
  84.2 1.6 %copy.12 = bf16[1,8,7168]{2,1,0:T(8,128)(2,1)} copy(bf16[1,8,7168]{2,1,0:T(8,128)(2,1)} %shard_map.73) | data formatting | bytes 229376

commit v3 on v2

--- a/solution.py
+++ b/solution.py
@@ -11,7 +11,7 @@
 MESH = pl.DeviceIdType.MESH
 LANES = 128
 LAG = 5
-AHEAD = 2
+AHEAD = 3
 
 
 def largest_divisor(value, most):

time: 86 us -> 88.7 us (1.031)
  Pallas kernels: 82.8 us -> 85.5 us
    pallas_call x1, Pallas kernels: 82.8 us -> 85.5 us  [local(): pl.pallas_call(functools.partial(kernel, count, unit_width, slots_gu, slo...]
where the time goes in v3:
time: 88.7 us; the launch traced here: 88.5 us
  Pallas kernels  85.5 us (96%)
  local copies, waits for them, and re-layouts  2.33 us (3%)
    pallas_call x1, Pallas kernels, local(): pl.pallas_call(functools.partial(kernel, count, unit_width, slots_gu, slo...  85.5 us
    unnamed x2, local copies, waits for them, and re-layouts  2.24 us

profile of v3, /device:TPU:0, one launch (start us, length us, event | category | flops | bytes accessed | tf_op | source)
XLA Modules:
  0.0 88.5 jit_solution(7397992101483748894)
XLA Ops:
  0.0 0.7 copy.10
  0.7 0.1 eq.15
  0.8 0.7 convert_reduce_fusion.hit
  1.4 85.5 %shard_map.73 = bf16[1,8,7168]{2,1,0:T(8,128)(2,1)} custom-call(bf16[2,8,7168]{2,1,0:T(8,128)(2,1)} %tokens.1, bf16[16,128]{1,0:T(8,128)(2,1)} %convert_reduce_fusion.hit, f32[1,7168]{1,0:T(1,128)} %gain.1, bf16[1,16,7168]{2,1,0:T(8,128)(2,1)} %bitcast.3, bf16[1,7168,2048]{2,1,0:T(8,128)(2,1)} %gate_hbm.1, bf16[1,7168,2048]{2,1,0:T(8,128)(2,1)} %up_hbm.1, ...), custom_call_target="tpu_custom_call" | custom-call | tf_op jit(solution)/shard_map/pallas_call | solution.py:338
  87.0 1.6 %copy.12 = bf16[1,8,7168]{2,1,0:T(8,128)(2,1)} copy(bf16[1,8,7168]{2,1,0:T(8,128)(2,1)} %shard_map.73) | data formatting | bytes 229376
